TPU v7x, 32 devices: a whole 2x2x4 slice. The times are simulated.
32 devices in a mesh: layer: 4 (over y, core), front: 8 (over z, x).
Axes of the slice: x: 2, y: 2, z: 4, core: 2. Of those that a mesh axis runs over, the one named last changes fastest.
Arguments:
- child_rhs: bfloat16 [4, 2, 48, 8192], P('layer', None, None, 'front'), may hold values from -6 to 6
- parent_rhs: bfloat16 [4, 2, 48, 4096], P('layer', None, None, 'front'), may hold values from -6 to 6
- root_rhs: bfloat16 [4, 2, 48, 4096], P('layer', None, None, 'front'), may hold values from -6 to 6
- child_inverse: bfloat16 [4, 2048, 8192], P('layer', None, 'front'), as said below
- child_update: bfloat16 [4, 8192, 2048], P('layer', 'front'), may hold values from -0.125 to 0.125
- parent_inverse: bfloat16 [4, 2048, 4096], P('layer', None, 'front'), as said below
- parent_update: bfloat16 [4, 4096, 3072], P('layer', 'front'), may hold values from -0.125 to 0.125
- root_inverse: bfloat16 [4, 4096, 4096], P('layer', None, 'front'), as said below
- coupling: float32 [4, 4096], P('layer', 'front'), may hold values from 0.25 to 1
- child_map: int32 [4, 2048], replicated, may hold values from 0 to 6143, as said below
- parent_map: int32 [2, 3072], replicated, may hold values from 0 to 4095, as said below
Outputs:
- solution: bfloat16 [4, 2, 48, 4096], P('layer', None, None, 'front')
Inputs may be any that keep to these rules, and one draw needn't show every extreme that they name: `child_map`: each row holds 2048 distinct entries; values below 2048 name rows of the parent front's separator, the others name row value - 2048 of the top separator. `parent_map`: each row holds 3072 distinct rows of the top separator. `child_inverse`: each group's matrix, read as rows k and columns f * 2048 + j, is zero where k > j. `parent_inverse`: each group's matrix, read as rows k and columns f * 2048 + j, is zero where k > j. `root_inverse`: each group's matrix is zero below its diagonal.
All inputs are finite; a program needn't handle non-finite values.
Results may differ from a plain program's by a relative error of at most 0.02.
Values may be sent and summed in bfloat16 or wider, within the bound.
No kernel may reach another device: no remote copies, remote signals or barrier semaphores. Data moves between devices by JAX's collectives and lax.ppermute only.
A program may use at most 64 MiB of HBM per device.

v0:
```python
import jax
import jax.numpy as jnp
from jax import lax
from jax.sharding import PartitionSpec as P

S0 = 4096


def partner_2(value, axis, apart):
    mask = 2**apart
    pairs = [(source, source ^ mask) for source in range(lax.axis_size(axis))]
    return lax.ppermute(value, axis, pairs)


def shifted(value, axis, steps):
    count = lax.axis_size(axis)
    first, last = (max(0, -steps), min(count, count - steps))
    return lax.ppermute(value, axis, [(source, source + steps) for source in range(first, last)])


def collect(shard, share_count, level_id):
    front_index = lax.axis_index("front")
    bit_count = share_count.bit_length() - 1
    joined = shard
    for bit_pos in range(bit_count):
        if level_id == 2:
            partner = partner_2(joined, "front", bit_pos)
        else:
            partner = partner_2(joined, "front", bit_pos)
        high_bit = front_index >> bit_pos & 1 == 1
        first_piece = jnp.where(high_bit, partner, joined)
        second_piece = jnp.where(high_bit, joined, partner)
        joined = jnp.concatenate([first_piece, second_piece], 1)
    return joined


def parent_updates(own_parent, parent_shares):
    front_index = lax.axis_index("front")
    buffer = lax.optimization_barrier(own_parent.astype(jnp.bfloat16)).astype(jnp.float32)
    bit_count = parent_shares.bit_length() - 1
    for bit_pos in reversed(range(bit_count)):
        half_width = buffer.shape[1] // 2
        lower_cols = buffer[:, :half_width]
        upper_cols = buffer[:, half_width:]
        upper_side = front_index >> bit_pos & 1 == 1
        sending = jnp.where(upper_side, lower_cols, upper_cols)
        partner = partner_2(sending.astype(jnp.bfloat16), "front", bit_pos).astype(sending.dtype)
        buffer = jnp.where(upper_side, upper_cols, lower_cols) + partner
    return buffer


def lower_levels(
    child_rhs,
    parent_rhs,
    child_inverse,
    child_update,
    parent_inverse,
    parent_update,
    child_map,
    parent_map,
):
    devices = lax.axis_size("front")
    front_index = lax.axis_index("front")
    child_shares = devices // 4
    parent_shares = devices // 2
    row_count = child_rhs.shape[0]
    parent_size = parent_inverse.shape[0]
    child_full = collect(child_rhs, child_shares, 2)
    child_solved = jnp.dot(child_full, child_inverse, preferred_element_type=jnp.float32).astype(
        jnp.bfloat16
    )
    child_terms = jnp.dot(child_solved, child_update, preferred_element_type=jnp.float32)
    child_front = front_index // child_shares
    targets = child_map[child_front]
    to_parent = jnp.where(targets < parent_size, targets, parent_size)
    to_root = jnp.where(targets >= parent_size, targets - parent_size, S0)
    own_parent = (
        jnp.zeros((row_count, parent_size), jnp.float32)
        .at[:, to_parent]
        .add(child_terms, mode="drop")
    )
    root_terms = (
        jnp.zeros((row_count, S0), jnp.float32).at[:, to_root].add(child_terms, mode="drop")
    )
    summed = parent_updates(own_parent, parent_shares)
    parent_now = (parent_rhs.astype(jnp.float32) - summed).astype(jnp.bfloat16)
    parent_full = collect(parent_now, parent_shares, 1)
    parent_solved = jnp.dot(parent_full, parent_inverse, preferred_element_type=jnp.float32).astype(
        jnp.bfloat16
    )
    parent_terms = jnp.dot(parent_solved, parent_update, preferred_element_type=jnp.float32)
    parent_targets = parent_map[front_index // parent_shares]
    return root_terms.at[:, parent_targets].add(parent_terms)


def root_level(root_terms, root_rhs, incoming, root_inverse, coupling):
    front_index = lax.axis_index("front")
    share_width = root_rhs.shape[1]
    own_cols = lax.dynamic_slice_in_dim(root_terms, front_index * share_width, share_width, 1)
    own_cols = own_cols + incoming.astype(jnp.float32) - root_rhs.astype(jnp.float32)
    root_total = lax.dynamic_update_slice_in_dim(root_terms, own_cols, front_index * share_width, 1)
    summed = lax.psum(root_total.astype(jnp.bfloat16), "front").astype(jnp.float32)
    root_now = (-summed).astype(jnp.bfloat16)
    root_solved = jnp.dot(root_now, root_inverse, preferred_element_type=jnp.float32)
    return (
        root_solved.astype(jnp.bfloat16),
        (coupling[None, :] * root_solved).astype(jnp.bfloat16),
    )


def body(
    child_rhs,
    parent_rhs,
    root_rhs,
    child_inverse,
    child_update,
    parent_inverse,
    parent_update,
    root_inverse,
    coupling,
    child_map,
    parent_map,
):
    row_count = child_rhs.shape[2]
    stacked_terms = lower_levels(
        child_rhs[0].reshape(2 * row_count, child_rhs.shape[3]),
        parent_rhs[0].reshape(2 * row_count, parent_rhs.shape[3]),
        child_inverse[0],
        child_update[0],
        parent_inverse[0],
        parent_update[0],
        child_map,
        parent_map,
    )
    first_terms = stacked_terms[:row_count]
    second_terms = stacked_terms[row_count:]
    silent = jnp.zeros_like(root_rhs[0, 0])
    first_sol, outgoing = root_level(
        first_terms, root_rhs[0, 0], silent, root_inverse[0], coupling[0]
    )
    incoming = shifted(outgoing, "layer", 1)
    second_sol, leftover = root_level(
        second_terms, root_rhs[0, 1], incoming, root_inverse[0], coupling[0]
    )
    return jnp.stack([first_sol, second_sol], axis=0)[None]


def solution(mesh):
    placed = (
        P("layer", None, None, "front"),
        P("layer", None, None, "front"),
        P("layer", None, None, "front"),
        P("layer", None, "front"),
        P("layer", "front", None),
        P("layer", None, "front"),
        P("layer", "front", None),
        P("layer", None, "front"),
        P("layer", "front"),
        P(),
        P(),
    )
    return jax.shard_map(
        body, mesh=mesh, in_specs=placed, out_specs=P("layer", None, None, "front"), check_vma=False
    )
```

profile of v0, /device:TPU:0, one launch (start us, length us, event | category | flops | bytes accessed | tf_op | source)
XLA Modules:
  0.0 282.1 jit_solution(15062157132926569334)
XLA Ops:
  6.5 3.0 %collective-permute-start = (bf16[96,1024]{1,0:T(8,128)(2,1)}, bf16[96,1024]{1,0:T(8,128)(2,1)}, u32[]{:S(2)}, u32[]{:S(2)}) collective-permute-start(bf16[96,1024]{1,0:T(8,128)(2,1)} %bitcast.67), channel_id=1, source_target_pairs={{0,1},{1,0},{2,3},{3,2},{4,5},{5,4},{6,7},{7,6},{8,9},{9,8},{10,11... | collective-permute-start | bytes 589832 | tf_op jit(solution)/shard_map/ppermute | solution.py:12
  10.9 3.8 %collective-permute-done = bf16[96,1024]{1,0:T(8,128)(2,1)} collective-permute-done((bf16[96,1024]{1,0:T(8,128)(2,1)}, bf16[96,1024]{1,0:T(8,128)(2,1)}, u32[]{:S(2)}, u32[]{:S(2)}) %collective-permute-start) | collective-permute-done | bytes 196640 | tf_op jit(solution)/shard_map/ppermute | solution.py:12
  15.8 5.8 %fusion.9 = f32[2048,96]{0,1:T(8,128)} fusion(bf16[1,1024,2048]{2,1,0:T(8,128)(2,1)} %param.15, bf16[1,2048,1024]{2,1,0:T(8,128)(2,1)} %param.14, bf16[96,1024]{1,0:T(8,128)(2,1)S(1)} %get-tuple-element.10, bf16[96,1024]{1,0:T(8,128)(2,1)S(1)} %get-tuple-element.9), kind=kOutput, calls=%fused_computation.13 | convolution fusion | flops 806191104 | bytes 9568256 | tf_op jit(solution)/shard_map/dot_general | solution.py:72
  21.6 2.5 copy.18
  24.1 12.8 %scatter_custom_fusion.1 = f32[96,2048]{0,1:T(8,128)} fusion(s32[2048]{0:T(1024)S(1)} %bitcast.70, f32[2048,96]{1,0:T(8,128)} %copy.18, f32[]{:T(128)} %constant.36.clone.1), kind=kCustom, calls=%fused_computation.29 | custom fusion | flops 196608 | bytes 786944 | tf_op jit(solution)/shard_map/scatter-add | solution.py:80
  38.3 1.9 collective-permute-start.1
  40.2 5.6 %collective-permute-done.1 = bf16[96,1024]{0,1:T(8,128)(2,1)S(1)} collective-permute-done((bf16[96,1024]{0,1:T(8,128)(2,1)S(1)}, bf16[96,1024]{0,1:T(8,128)(2,1)S(1)}, u32[]{:S(2)}, u32[]{:S(2)}) %collective-permute-start.1) | collective-permute-done | bytes 196640 | tf_op jit(solution)/shard_map/ppermute | solution.py:12
  50.0 1.9 collective-permute-done.2
  51.9 1.8 subtract_convert_fusion
  56.1 2.9 %collective-permute-done.3 = bf16[96,512]{0,1:T(8,128)(2,1)} collective-permute-done((bf16[96,512]{0,1:T(8,128)(2,1)}, bf16[96,512]{0,1:T(8,128)(2,1)}, u32[]{:S(2)}, u32[]{:S(2)}) %collective-permute-start.3) | collective-permute-done | bytes 98336 | tf_op jit(solution)/shard_map/ppermute | solution.py:12
  63.0 13.3 %scatter_custom_fusion = f32[96,4096]{0,1:T(8,128)} fusion(s32[2048]{0:T(1024)} %bitcast.69, f32[2048,96]{1,0:T(8,128)} %copy.18, f32[]{:T(128)} %constant.36.clone.1), kind=kCustom, calls=%fused_computation.21 | custom fusion | flops 196608 | bytes 1573376 | tf_op jit(solution)/shard_map/scatter-add | solution.py:83
  76.3 1.9 broadcast_select_fusion.1
  78.1 3.9 %convolution_bitcast_fusion = f32[3072,96]{0,1:T(8,128)} fusion(bf16[1,512,3072]{2,1,0:T(8,128)(2,1)S(1)} %copy-done, bf16[1,2048,512]{2,1,0:T(8,128)(2,1)} %param.16, bf16[96,1024]{0,1:T(8,128)(2,1)} %get-tuple-element.8, bf16[96,1024]{0,1:T(8,128)(2,1)} %get-tuple-element.7), kind=kOutput, calls=%fused_computation.11 | convolution fusion | flops 504152064 | bytes 6815744 | tf_op jit(solution)/shard_map/dot_general | solution.py:91
  82.0 2.9 %copy.21 = f32[3072,96]{1,0:T(8,128)} copy(f32[3072,96]{0,1:T(8,128)} %convolution_bitcast_fusion) | data formatting | bytes 2359296 | tf_op jit(solution)/shard_map/dot_general | solution.py:91
  84.9 18.5 %scatter_fusion = f32[96,4096]{0,1:T(8,128)} fusion(f32[96,4096]{0,1:T(8,128)} %scatter_custom_fusion, s32[3072]{0:T(1024)S(1)} %bitcast.68, f32[3072,96]{1,0:T(8,128)} %copy.21), kind=kCustom, calls=%fused_computation.2 | custom fusion | flops 294912 | bytes 3551232 | tf_op jit(solution)/shard_map/scatter-add | solution.py:93
  103.4 4.2 %fusion.52 = (f32[48,4096]{0,1:T(8,128)S(1)}, f32[48,4096]{0,1:T(8,128)}) fusion(f32[96,4096]{0,1:T(8,128)} %scatter_fusion), kind=kLoop, calls=%fused_computation.59 | loop fusion | bytes 3145728 | tf_op jit(solution)/shard_map/slice | solution.py:135
  108.8 78.7 %all-reduce.3.cloned.1.call-done = bf16[48,4096]{0,1:T(8,128)(2,1)} async-done(((bf16[48,4096]{0,1:T(8,128)(2,1)}), bf16[48,4096]{0,1:T(8,128)(2,1)}) %all-reduce.3.cloned.1.call-update) | async-done | bytes 393232 | tf_op jit(solution)/shard_map/psum | solution.py:102
  187.5 3.4 %convert_bitcast_fusion = (bf16[1,48,512]{2,1,0:T(8,128)(2,1)S(1)}, bf16[48,512]{1,0:T(8,128)(2,1)S(1)}) fusion(f32[512]{0:T(512)S(1)} %bitcast.71, bf16[1,4096,512]{2,1,0:T(8,128)(2,1)} %param.18, bf16[48,4096]{0,1:T(8,128)(2,1)} %all-reduce.3.cloned.1.call-done), kind=kOutput, calls=%fused_computation.51 | convolution fusion | flops 201990144 | bytes 4687872 | tf_op jit(solution)/shard_map/dot_general | solution.py:104
  190.9 1.8 collective-permute-start.5
  192.7 3.1 %copy.25 = f32[48,4096]{1,0:T(8,128)} copy(f32[48,4096]{0,1:T(8,128)} %get-tuple-element.6) | data formatting | bytes 1572864
  195.8 1.6 fusion.47
  197.3 1.9 convert_element_type.96
  199.3 72.2 %all-reduce.5.cloned.1.call-done = bf16[48,4096]{1,0:T(8,128)(2,1)} async-done(((bf16[48,4096]{1,0:T(8,128)(2,1)}), bf16[48,4096]{1,0:T(8,128)(2,1)}) %all-reduce.5.cloned.1.call-update) | async-done | bytes 393232 | tf_op jit(solution)/shard_map/psum | solution.py:102
  271.5 3.1 %fusion.25 = bf16[1,48,512]{2,1,0:T(8,128)(2,1)S(1)} fusion(bf16[1,4096,512]{2,1,0:T(8,128)(2,1)} %param.18, bf16[48,4096]{1,0:T(8,128)(2,1)} %all-reduce.5.cloned.1.call-done), kind=kOutput, calls=%fused_computation.20 | convolution fusion | flops 201940992 | bytes 4636672 | tf_op jit(solution)/shard_map/dot_general | solution.py:104
  (36 shorter events, 16.4 us)
Async XLA Ops:
  6.5 71.6 %copy-start = (bf16[1,512,3072]{2,1,0:T(8,128)(2,1)S(1)}, bf16[1,512,3072]{2,1,0:T(8,128)(2,1)}, u32[]{:S(2)}) copy-start(bf16[1,512,3072]{2,1,0:T(8,128)(2,1)} %param.17) | copy-start | bytes 9437188
  6.5 180.9 %all-reduce.3.cloned.1.call-start = ((), (), s32[]{:S(2)}) async-start(), calls=%async_computation | async-start | bytes 2097152 | tf_op jit(solution)/shard_map/psum | solution.py:102
  6.5 8.2 %collective-permute-start = (bf16[96,1024]{1,0:T(8,128)(2,1)}, bf16[96,1024]{1,0:T(8,128)(2,1)}, u32[]{:S(2)}, u32[]{:S(2)}) collective-permute-start(bf16[96,1024]{1,0:T(8,128)(2,1)} %bitcast.67), channel_id=1, source_target_pairs={{0,1},{1,0},{2,3},{3,2},{4,5},{5,4},{6,7},{7,6},{8,9},{9,8},{10,11... | collective-permute-start | bytes 589832 | tf_op jit(solution)/shard_map/ppermute | solution.py:12
  38.2 10.1 %copy-start.3 = (bf16[1,2,48,512]{3,2,1,0:T(8,128)(2,1)S(1)}, bf16[1,2,48,512]{3,2,1,0:T(8,128)(2,1)}, u32[]{:S(2)}) copy-start(bf16[1,2,48,512]{3,2,1,0:T(8,128)(2,1)} %param.12) | copy-start | bytes 294916
  38.3 7.5 %collective-permute-start.1 = (bf16[96,1024]{0,1:T(8,128)(2,1)S(1)}, bf16[96,1024]{0,1:T(8,128)(2,1)S(1)}, u32[]{:S(2)}, u32[]{:S(2)}) collective-permute-start(bf16[96,1024]{0,1:T(8,128)(2,1)S(1)} %select_convert_fusion), channel_id=1, source_target_pairs={{0,2},{1,3},{2,0},{3,1},{4,6},{5,7},{6,4},{7,5},{8,10},{9,11},{10,... | collective-permute-start | bytes 589832 | tf_op jit(solution)/shard_map/ppermute | solution.py:12
  45.9 0.8 copy-start.1
  46.7 5.1 %collective-permute-start.2 = (bf16[96,512]{0,1:T(8,128)(2,1)S(1)}, bf16[96,512]{0,1:T(8,128)(2,1)}, u32[]{:S(2)}, u32[]{:S(2)}) collective-permute-start(bf16[96,512]{0,1:T(8,128)(2,1)S(1)} %select_convert_fusion.1), channel_id=1, source_target_pairs={{0,1},{1,0},{2,3},{3,2},{4,5},{5,4},{6,7},{7,6},{8,9},{9,8},{10,11... | collective-permute-start | bytes 294920 | tf_op jit(solution)/shard_map/ppermute | solution.py:12
  53.7 5.3 %collective-permute-start.3 = (bf16[96,512]{0,1:T(8,128)(2,1)}, bf16[96,512]{0,1:T(8,128)(2,1)}, u32[]{:S(2)}, u32[]{:S(2)}) collective-permute-start(bf16[96,512]{0,1:T(8,128)(2,1)} %subtract_convert_fusion), channel_id=1, source_target_pairs={{0,1},{1,0},{2,3},{3,2},{4,5},{5,4},{6,7},{7,6},{8,9},{9,8},{10,11... | collective-permute-start | bytes 294920 | tf_op jit(solution)/shard_map/ppermute | solution.py:12
  60.7 15.6 %collective-permute-start.4 = (bf16[96,1024]{0,1:T(8,128)(2,1)}, bf16[96,1024]{0,1:T(8,128)(2,1)}, u32[]{:S(2)}, u32[]{:S(2)}) collective-permute-start(bf16[96,1024]{0,1:T(8,128)(2,1)} %pad_maximum_fusion), channel_id=1, source_target_pairs={{0,2},{1,3},{2,0},{3,1},{4,6},{5,7},{6,4},{7,5},{8,10},{9,11},{10,... | collective-permute-start | bytes 589832 | tf_op jit(solution)/shard_map/ppermute | solution.py:12
  107.6 79.9 %copy-start.4 = (f32[1,512]{1,0:T(1,128)S(1)}, f32[1,512]{1,0:T(1,128)}, u32[]{:S(2)}) copy-start(f32[1,512]{1,0:T(1,128)} %param.19) | copy-start | bytes 6148
  108.7 162.7 %all-reduce.5.cloned.1.call-start = ((), (), s32[]{:S(2)}) async-start(), calls=%async_computation.1 | async-start | bytes 786432 | tf_op jit(solution)/shard_map/psum | solution.py:102
  190.9 4.9 %copy-start.2 = (bf16[1,2,48,512]{3,2,1,0:T(8,128)(2,1)S(1)}, bf16[1,2,48,512]{3,2,1,0:T(8,128)(2,1)}, u32[]{:S(2)}) copy-start(bf16[1,2,48,512]{3,2,1,0:T(8,128)(2,1)} %param.13) | copy-start | bytes 294916
  190.9 4.9 %collective-permute-start.5 = (bf16[48,512]{1,0:T(8,128)(2,1)S(1)}, bf16[48,512]{1,0:T(8,128)(2,1)S(1)}, u32[]{:S(2)}, u32[]{:S(2)}) collective-permute-start(bf16[48,512]{1,0:T(8,128)(2,1)S(1)} %get-tuple-element.14), channel_id=1, source_target_pairs={{0,8},{8,16},{16,24},{1,9},{9,17},{17,25},{2,10},{10,18},{18,26},{... | collective-permute-start | bytes 147464 | tf_op jit(solution)/shard_map/ppermute | solution.py:18
Sparse Core Ops, SparseCore 0:
  108.9 78.5 all-reduce.2
  199.4 72.0 all-reduce.4
where the time goes:
time: 283 us; the launch traced here: 282 us
  waiting for transfers between devices  165 us (58%)
  other arithmetic  60.6 us (21%)
  matrix products  16.2 us (6%)
  local copies, waits for them, and re-layouts  15.3 us (5%)
  between operations  13.5 us (5%)
  starting transfers between devices  11.3 us (4%)
    psum x2, waiting for transfers between devices, root_level(): lax.psum(root_total.astype(jnp.bfloat16), 'front').astype(jnp.float32)  151 us
    scatter-add x1, other arithmetic, lower_levels(): return root_terms.at[:, parent_targets].add(parent_terms)  18.5 us
    ppermute x5, waiting for transfers between devices, partner_2(): return lax.ppermute(value, axis, pairs)  14.2 us
    scatter-add x1, other arithmetic, lower_levels(): jnp.zeros((row_count, S0), jnp.float32).at[:, to_root]  13.3 us
    scatter-add x1, other arithmetic, lower_levels(): own_parent = jnp.zeros((row_count, parent_size), jnp.float32).at[:, to_pa...  12.8 us
    ppermute x5, starting transfers between devices, partner_2(): return lax.ppermute(value, axis, pairs)  9.41 us
    dot_general x2, matrix products, root_level(): jnp.dot(root_now, root_inverse, preferred_element_type=jnp.float32)  6.52 us
    dot_general x1, matrix products, lower_levels(): jnp.dot(child_solved, child_update, preferred_element_type=jnp.float32)  5.84 us
  transfers between devices with their start and end apart: 8, of which 6 were waited for; matrix products, arithmetic and copies ran while one was open for 7% of the time, Pallas kernels for 0%

commit v1 on v0

--- a/solution.py
+++ b/solution.py
@@ -99,7 +99,9 @@
     own_cols = lax.dynamic_slice_in_dim(root_terms, front_index * share_width, share_width, 1)
     own_cols = own_cols + incoming.astype(jnp.float32) - root_rhs.astype(jnp.float32)
     root_total = lax.dynamic_update_slice_in_dim(root_terms, own_cols, front_index * share_width, 1)
-    summed = lax.psum(root_total.astype(jnp.bfloat16), "front").astype(jnp.float32)
+    summed = jnp.sum(lax.all_gather(root_total.astype(jnp.bfloat16), "front"), axis=0).astype(
+        jnp.float32
+    )
     root_now = (-summed).astype(jnp.bfloat16)
     root_solved = jnp.dot(root_now, root_inverse, preferred_element_type=jnp.float32)
     return (

time: 283 us -> 262 us (0.926)
  waiting for transfers between devices: 165 us -> 136 us
  other arithmetic: 60.6 us -> 66.4 us
  local copies, waits for them, and re-layouts: 15.3 us -> 18.2 us
    psum x2 -> x0, waiting for transfers between devices: 151 us -> none  [root_level(): lax.psum(root_total.astype(jnp.bfloat16), 'front').astype(jnp.float32)]
    all_gather x0 -> x2, waiting for transfers between devices: none -> 120 us  [root_level(): lax.all_gather(root_total.astype(jnp.bfloat16), 'front')]
    reduce_sum x0 -> x2, other arithmetic: none -> 4.76 us  [root_level(): jnp.sum(lax.all_gather(root_total.astype(jnp.bfloat16), 'front'), axis=0)]
    unnamed x12 -> x16, local copies, waits for them, and re-layouts: 4 us -> 6.95 us
where the time goes in v1:
time: 262 us; the launch traced here: 261 us
  waiting for transfers between devices  136 us (52%)
  other arithmetic  66.4 us (25%)
  local copies, waits for them, and re-layouts  18.2 us (7%)
  matrix products  16.4 us (6%)
  between operations  13.5 us (5%)
  starting transfers between devices  10.9 us (4%)
    all_gather x2, waiting for transfers between devices, root_level(): lax.all_gather(root_total.astype(jnp.bfloat16), 'front')  120 us
    scatter-add x1, other arithmetic, lower_levels(): return root_terms.at[:, parent_targets].add(parent_terms)  18.5 us
    ppermute x5, waiting for transfers between devices, partner_2(): return lax.ppermute(value, axis, pairs)  15.5 us
    scatter-add x1, other arithmetic, lower_levels(): jnp.zeros((row_count, S0), jnp.float32).at[:, to_root]  13.2 us
    scatter-add x1, other arithmetic, lower_levels(): own_parent = jnp.zeros((row_count, parent_size), jnp.float32).at[:, to_pa...  12.8 us
    ppermute x5, starting transfers between devices, partner_2(): return lax.ppermute(value, axis, pairs)  9.47 us
    unnamed x16, local copies, waits for them, and re-layouts  6.95 us
    dot_general x2, matrix products, root_level(): jnp.dot(root_now, root_inverse, preferred_element_type=jnp.float32)  6.7 us
  transfers between devices with their start and end apart: 8, of which 6 were waited for; matrix products, arithmetic and copies ran while one was open for 7% of the time, Pallas kernels for 0%

profile of v1, /device:TPU:0, one launch (start us, length us, event | category | flops | bytes accessed | tf_op | source)
XLA Modules:
  0.0 261.5 jit_solution(10639645892304315236)
XLA Ops:
  6.5 3.0 %collective-permute-start = (bf16[96,1024]{1,0:T(8,128)(2,1)}, bf16[96,1024]{1,0:T(8,128)(2,1)}, u32[]{:S(2)}, u32[]{:S(2)}) collective-permute-start(bf16[96,1024]{1,0:T(8,128)(2,1)} %bitcast.71), channel_id=1, source_target_pairs={{0,1},{1,0},{2,3},{3,2},{4,5},{5,4},{6,7},{7,6},{8,9},{9,8},{10,11... | collective-permute-start | bytes 589832 | tf_op jit(solution)/shard_map/ppermute | solution.py:12
  10.3 4.4 %collective-permute-done = bf16[96,1024]{1,0:T(8,128)(2,1)} collective-permute-done((bf16[96,1024]{1,0:T(8,128)(2,1)}, bf16[96,1024]{1,0:T(8,128)(2,1)}, u32[]{:S(2)}, u32[]{:S(2)}) %collective-permute-start) | collective-permute-done | bytes 196640 | tf_op jit(solution)/shard_map/ppermute | solution.py:12
  15.8 5.8 %fusion.9 = f32[2048,96]{0,1:T(8,128)} fusion(bf16[1,1024,2048]{2,1,0:T(8,128)(2,1)} %param.15, bf16[1,2048,1024]{2,1,0:T(8,128)(2,1)} %param.14, bf16[96,1024]{1,0:T(8,128)(2,1)S(1)} %get-tuple-element.10, bf16[96,1024]{1,0:T(8,128)(2,1)S(1)} %get-tuple-element.9), kind=kOutput, calls=%fused_computation.13 | convolution fusion | flops 806191104 | bytes 9568256 | tf_op jit(solution)/shard_map/dot_general | solution.py:72
  21.6 2.5 copy.32
  24.1 12.8 %scatter_custom_fusion.1 = f32[96,2048]{0,1:T(8,128)} fusion(s32[2048]{0:T(1024)S(1)} %bitcast.74, f32[2048,96]{1,0:T(8,128)} %copy.32, f32[]{:T(128)} %constant.39.clone.1), kind=kCustom, calls=%fused_computation.29 | custom fusion | flops 196608 | bytes 786944 | tf_op jit(solution)/shard_map/scatter-add | solution.py:80
  38.3 1.9 collective-permute-start.1
  40.2 5.6 %collective-permute-done.1 = bf16[96,1024]{0,1:T(8,128)(2,1)S(1)} collective-permute-done((bf16[96,1024]{0,1:T(8,128)(2,1)S(1)}, bf16[96,1024]{0,1:T(8,128)(2,1)S(1)}, u32[]{:S(2)}, u32[]{:S(2)}) %collective-permute-start.1) | collective-permute-done | bytes 196640 | tf_op jit(solution)/shard_map/ppermute | solution.py:12
  54.6 3.6 %collective-permute-done.3 = bf16[96,512]{0,1:T(8,128)(2,1)} collective-permute-done((bf16[96,512]{0,1:T(8,128)(2,1)S(1)}, bf16[96,512]{0,1:T(8,128)(2,1)}, u32[]{:S(2)}, u32[]{:S(2)}) %collective-permute-start.3) | collective-permute-done | bytes 98336 | tf_op jit(solution)/shard_map/ppermute | solution.py:12
  62.2 13.2 %scatter_custom_fusion = f32[96,4096]{0,1:T(8,128)} fusion(s32[2048]{0:T(1024)S(1)} %bitcast.73, f32[2048,96]{1,0:T(8,128)} %copy.32, f32[]{:T(128)} %constant.39.clone.1), kind=kCustom, calls=%fused_computation.20 | custom fusion | flops 196608 | bytes 1573376 | tf_op jit(solution)/shard_map/scatter-add | solution.py:83
  75.4 1.9 broadcast_select_fusion.1
  77.3 3.9 %convolution_bitcast_fusion = f32[3072,96]{0,1:T(8,128)} fusion(bf16[1,512,3072]{2,1,0:T(8,128)(2,1)S(1)} %copy-done, bf16[1,2048,512]{2,1,0:T(8,128)(2,1)} %param.16, bf16[96,1024]{0,1:T(8,128)(2,1)} %get-tuple-element.8, bf16[96,1024]{0,1:T(8,128)(2,1)} %get-tuple-element.7), kind=kOutput, calls=%fused_computation.11 | convolution fusion | flops 504152064 | bytes 6815744 | tf_op jit(solution)/shard_map/dot_general | solution.py:91
  81.2 2.9 %copy.35 = f32[3072,96]{1,0:T(8,128)} copy(f32[3072,96]{0,1:T(8,128)} %convolution_bitcast_fusion) | data formatting | bytes 2359296 | tf_op jit(solution)/shard_map/dot_general | solution.py:91
  84.1 18.5 %scatter_fusion = f32[96,4096]{0,1:T(8,128)} fusion(f32[96,4096]{0,1:T(8,128)} %scatter_custom_fusion, s32[3072]{0:T(1024)S(1)} %bitcast.72, f32[3072,96]{1,0:T(8,128)} %copy.35), kind=kCustom, calls=%fused_computation.2 | custom fusion | flops 294912 | bytes 3551232 | tf_op jit(solution)/shard_map/scatter-add | solution.py:93
  102.6 4.8 %fusion.52 = (f32[48,4096]{0,1:T(8,128)}, f32[48,4096]{0,1:T(8,128)}) fusion(f32[96,4096]{0,1:T(8,128)} %scatter_fusion), kind=kLoop, calls=%fused_computation.59 | loop fusion | bytes 3145728 | tf_op jit(solution)/shard_map/slice | solution.py:137
  107.4 3.1 %copy.38 = f32[48,4096]{1,0:T(8,128)} copy(f32[48,4096]{0,1:T(8,128)} %get-tuple-element.5) | data formatting | bytes 1572864
  112.0 2.0 convert_element_type.92
  114.1 60.4 %all-gather.5.cloned.1.call-done = bf16[384,4096]{1,0:T(8,128)(2,1)} async-done(((bf16[48,4096]{1,0:T(8,128)(2,1)}), bf16[384,4096]{1,0:T(8,128)(2,1)}) %all-gather.5.cloned.1.call-update) | async-done | bytes 3145744 | tf_op jit(solution)/shard_map/all_gather | solution.py:102
  174.4 2.4 reduce_sum.24
  176.8 3.7 %convert_bitcast_fusion = (bf16[1,48,512]{2,1,0:T(8,128)(2,1)}, bf16[48,512]{1,0:T(8,128)(2,1)}) fusion(f32[512]{0:T(512)S(1)} %bitcast.75, bf16[1,4096,512]{2,1,0:T(8,128)(2,1)} %param.18, bf16[48,4096]{1,0:T(8,128)(2,1)S(1)} %reduce_sum.24), kind=kOutput, calls=%fused_computation.51 | convolution fusion | flops 201990144 | bytes 4687872 | tf_op jit(solution)/shard_map/dot_general | solution.py:106
  181.9 3.1 %copy.39 = f32[48,4096]{1,0:T(8,128)} copy(f32[48,4096]{0,1:T(8,128)} %get-tuple-element.6) | data formatting | bytes 1572864
  186.5 1.9 convert_element_type.100
  188.5 60.1 %all-gather.7.cloned.1.call-done = bf16[384,4096]{1,0:T(8,128)(2,1)} async-done(((bf16[48,4096]{1,0:T(8,128)(2,1)}), bf16[384,4096]{1,0:T(8,128)(2,1)}) %all-gather.7.cloned.1.call-update) | async-done | bytes 3145744 | tf_op jit(solution)/shard_map/all_gather | solution.py:102
  248.6 2.4 reduce_sum.25
  251.0 3.0 %fusion.25 = bf16[1,48,512]{2,1,0:T(8,128)(2,1)S(1)} fusion(bf16[1,4096,512]{2,1,0:T(8,128)(2,1)} %param.18, bf16[48,4096]{1,0:T(8,128)(2,1)S(1)} %reduce_sum.25), kind=kOutput, calls=%fused_computation.19 | convolution fusion | flops 201940992 | bytes 4636672 | tf_op jit(solution)/shard_map/dot_general | solution.py:106
  (41 shorter events, 21.2 us)
Async XLA Ops:
  6.5 70.8 %copy-start = (bf16[1,512,3072]{2,1,0:T(8,128)(2,1)S(1)}, bf16[1,512,3072]{2,1,0:T(8,128)(2,1)}, u32[]{:S(2)}) copy-start(bf16[1,512,3072]{2,1,0:T(8,128)(2,1)} %param.17) | copy-start | bytes 9437188
  6.5 167.9 %all-gather.5.cloned.1.call-start = ((), (), s32[]{:S(2)}) async-start(), calls=%async_computation | async-start | bytes 3538944 | tf_op jit(solution)/shard_map/all_gather | solution.py:102
  6.5 8.2 %collective-permute-start = (bf16[96,1024]{1,0:T(8,128)(2,1)}, bf16[96,1024]{1,0:T(8,128)(2,1)}, u32[]{:S(2)}, u32[]{:S(2)}) collective-permute-start(bf16[96,1024]{1,0:T(8,128)(2,1)} %bitcast.71), channel_id=1, source_target_pairs={{0,1},{1,0},{2,3},{3,2},{4,5},{5,4},{6,7},{7,6},{8,9},{9,8},{10,11... | collective-permute-start | bytes 589832 | tf_op jit(solution)/shard_map/ppermute | solution.py:12
  38.2 10.1 %copy-start.3 = (bf16[1,2,48,512]{3,2,1,0:T(8,128)(2,1)S(1)}, bf16[1,2,48,512]{3,2,1,0:T(8,128)(2,1)}, u32[]{:S(2)}) copy-start(bf16[1,2,48,512]{3,2,1,0:T(8,128)(2,1)} %param.12) | copy-start | bytes 294916
  38.3 7.5 %collective-permute-start.1 = (bf16[96,1024]{0,1:T(8,128)(2,1)S(1)}, bf16[96,1024]{0,1:T(8,128)(2,1)S(1)}, u32[]{:S(2)}, u32[]{:S(2)}) collective-permute-start(bf16[96,1024]{0,1:T(8,128)(2,1)S(1)} %select_convert_fusion), channel_id=1, source_target_pairs={{0,2},{1,3},{2,0},{3,1},{4,6},{5,7},{6,4},{7,5},{8,10},{9,11},{10,... | collective-permute-start | bytes 589832 | tf_op jit(solution)/shard_map/ppermute | solution.py:12
  45.9 0.8 copy-start.1
  46.7 5.1 %collective-permute-start.2 = (bf16[96,512]{0,1:T(8,128)(2,1)S(1)}, bf16[96,512]{0,1:T(8,128)(2,1)}, u32[]{:S(2)}, u32[]{:S(2)}) collective-permute-start(bf16[96,512]{0,1:T(8,128)(2,1)S(1)} %select_convert_fusion.1), channel_id=1, source_target_pairs={{0,1},{1,0},{2,3},{3,2},{4,5},{5,4},{6,7},{7,6},{8,9},{9,8},{10,11... | collective-permute-start | bytes 294920 | tf_op jit(solution)/shard_map/ppermute | solution.py:12
  53.0 5.1 %collective-permute-start.3 = (bf16[96,512]{0,1:T(8,128)(2,1)S(1)}, bf16[96,512]{0,1:T(8,128)(2,1)}, u32[]{:S(2)}, u32[]{:S(2)}) collective-permute-start(bf16[96,512]{0,1:T(8,128)(2,1)S(1)} %subtract_convert_fusion), channel_id=1, source_target_pairs={{0,1},{1,0},{2,3},{3,2},{4,5},{5,4},{6,7},{7,6},{8,9},{9,8},{10,11... | collective-permute-start | bytes 294920 | tf_op jit(solution)/shard_map/ppermute | solution.py:12
  59.8 15.6 %collective-permute-start.4 = (bf16[96,1024]{0,1:T(8,128)(2,1)}, bf16[96,1024]{0,1:T(8,128)(2,1)}, u32[]{:S(2)}, u32[]{:S(2)}) collective-permute-start(bf16[96,1024]{0,1:T(8,128)(2,1)} %pad_maximum_fusion), channel_id=1, source_target_pairs={{0,2},{1,3},{2,0},{3,1},{4,6},{5,7},{6,4},{7,5},{8,10},{9,11},{10,... | collective-permute-start | bytes 589832 | tf_op jit(solution)/shard_map/ppermute | solution.py:12
  107.4 3.1 %copy-start.4 = (bf16[1,2,48,512]{3,2,1,0:T(8,128)(2,1)S(1)}, bf16[1,2,48,512]{3,2,1,0:T(8,128)(2,1)}, u32[]{:S(2)}) copy-start(bf16[1,2,48,512]{3,2,1,0:T(8,128)(2,1)} %param.13) | copy-start | bytes 294916
  114.0 62.8 %copy-start.6 = (f32[1,512]{1,0:T(1,128)S(1)}, f32[1,512]{1,0:T(1,128)}, u32[]{:S(2)}) copy-start(f32[1,512]{1,0:T(1,128)} %param.19) | copy-start | bytes 6148
  114.0 134.5 %all-gather.7.cloned.1.call-start = ((), (), s32[]{:S(2)}) async-start(), calls=%async_computation.1 | async-start | bytes 3538944 | tf_op jit(solution)/shard_map/all_gather | solution.py:102
  180.5 4.5 %copy-start.5 = (bf16[1,2,48,512]{3,2,1,0:T(8,128)(2,1)S(1)}, bf16[1,2,48,512]{3,2,1,0:T(8,128)(2,1)}, u32[]{:S(2)}) copy-start(bf16[1,2,48,512]{3,2,1,0:T(8,128)(2,1)} %param.13) | copy-start | bytes 294916
  180.5 4.5 %collective-permute-start.5 = (bf16[48,512]{1,0:T(8,128)(2,1)}, bf16[48,512]{1,0:T(8,128)(2,1)S(1)}, u32[]{:S(2)}, u32[]{:S(2)}) collective-permute-start(bf16[48,512]{1,0:T(8,128)(2,1)} %get-tuple-element.14), channel_id=1, source_target_pairs={{0,8},{8,16},{16,24},{1,9},{9,17},{17,25},{2,10},{10,18},{18,26},{... | collective-permute-start | bytes 147464 | tf_op jit(solution)/shard_map/ppermute | solution.py:18
  250.9 3.0 %copy-start.2 = (bf16[1,48,512]{2,1,0:T(8,128)(2,1)S(1)}, bf16[1,48,512]{2,1,0:T(8,128)(2,1)}, u32[]{:S(2)}) copy-start(bf16[1,48,512]{2,1,0:T(8,128)(2,1)} %get-tuple-element.13) | copy-start | bytes 147460
Sparse Core Ops, SparseCore 0:
  114.1 60.2 all-gather.4
  188.6 59.9 all-gather.6
